TPU v7x, 128 devices: a whole 4x4x4 slice. The times are simulated.
128 devices in a mesh: leaf: 16 (over x, z), panel: 8 (over y, core).
Axes of the slice: x: 4, y: 4, z: 4, core: 2. Of those that a mesh axis runs over, the one named last changes fastest.
Arguments:
- adjoint_rhs: float32 [16, 64, 3968], P('leaf', None, 'panel'), may hold values from -6 to 6
- panel_tiles: bfloat16 [16, 2048, 12544], P('leaf', 'panel'), may hold values from -0.0625 to 0.0625
- diag_inverse: bfloat16 [16, 3968, 2048], P('leaf', 'panel'), may hold values from -0.125 to 0.125
- front_sizes: int32 [31], replicated, may hold values from 512 to 2048
Outputs:
- solution: float32 [16, 5, 64, 2048], P('leaf', None, None, 'panel')
All inputs are finite; a program needn't handle non-finite values.
Results may differ from a plain program's by a relative error of at most 0.0051.
Values sent between devices are 32-bit elements; how exact they have to be, the bound alone decides.
A program may use at most 128 MiB of HBM per device.

v0:
```python
import jax
import jax.numpy as jnp
from jax import lax
from jax.sharding import PartitionSpec as P


def per_device(adjoint_rhs, panel_tiles, diag_inverse, front_sizes):
    leaf_count = lax.axis_size("leaf")
    panel_count = lax.axis_size("panel")
    levels = leaf_count.bit_length()
    leaf_pos = lax.axis_index("leaf")
    panel_pos = lax.axis_index("panel")
    sep_rows = diag_inverse.shape[2]
    strip = panel_tiles.shape[1]
    columns = jnp.arange(sep_rows)
    solved = []
    results = []
    for height in range(levels):
        group_size = leaf_count >> height
        col_width = sep_rows // group_size
        share = col_width // panel_count
        col_start = sum((upper * (sep_rows // (leaf_count >> upper)) for upper in range(height)))
        row_start = sum(
            (sep_rows // (leaf_count >> upper) // panel_count for upper in range(height))
        )
        front_pos = leaf_pos // group_size
        member = leaf_pos % group_size
        right = adjoint_rhs[0, :, row_start : row_start + share]
        if height > 0:
            strips = jnp.stack([solved[upper] for upper in range(height)], axis=1)
            region = panel_tiles[0, :, col_start : col_start + height * col_width].reshape(
                strip, height, col_width
            )
            partial_value = jnp.einsum(
                "nar,raw->nw", strips, region, preferred_element_type=jnp.float32
            )
            shares = lax.psum_scatter(partial_value, "panel", scatter_dimension=1, tiled=True)
            resid = right - shares
        else:
            resid = right
        front_id = (1 << height) - 1 + front_pos
        live_size = jnp.sum(jnp.where(jnp.arange(front_sizes.shape[0]) == front_id, front_sizes, 0))
        global_rows = member * col_width + panel_pos * share + jnp.arange(share)
        resid_low = jnp.where(global_rows[None, :] < live_size, resid, 0.0).astype(jnp.bfloat16)
        block = diag_inverse[0, row_start : row_start + share, :].astype(jnp.float32)
        below = columns[None, :] <= global_rows[:, None]
        factor = (
            jnp.where(below, block, 0.0)
            + (columns[None, :] == global_rows[:, None]).astype(jnp.float32)
        ).astype(jnp.bfloat16)
        terms = jnp.dot(resid_low, factor, preferred_element_type=jnp.float32)
        slots = jnp.zeros((leaf_count // group_size,) + terms.shape, jnp.float32)
        slots = lax.dynamic_update_index_in_dim(slots, terms, front_pos, 0)
        summed = lax.psum(slots, ("leaf", "panel"))
        total = lax.dynamic_index_in_dim(summed, front_pos, 0, keepdims=False)
        mine = lax.dynamic_slice_in_dim(total, panel_pos * strip, strip, 1)
        rows_now = mine.astype(jnp.bfloat16)
        solved.append(rows_now)
        results.append(mine)
    return jnp.stack(results, axis=0)[None]


def solution(mesh):
    in_specs = (P("leaf", None, "panel"), P("leaf", "panel", None), P("leaf", "panel", None), P())
    out_specs = P("leaf", None, None, "panel")
    return jax.shard_map(
        per_device, mesh=mesh, in_specs=in_specs, out_specs=out_specs, check_vma=False
    )
```

profile of v0, /device:TPU:1, one launch (start us, length us, event | category | flops | bytes accessed | tf_op | source)
XLA Modules:
  0.0 927.9 jit_solution(10410377845542587859)
XLA Ops:
  6.5 1.5 fusion.88
  8.7 1.9 convolution_bitcast_fusion
  10.7 150.0 %all-reduce.6.cloned.1.call-done = f32[1,64,2048]{2,1,0:T(8,128)} async-done(((f32[1,64,2048]{2,1,0:T(8,128)}), f32[1,64,2048]{2,1,0:T(8,128)}) %all-reduce.6.cloned.1.call-update) | async-done | bytes 524304 | tf_op jit(solution)/shard_map/psum | solution.py:54
  160.7 1.8 convolution_bitcast_fusion.8
  163.3 26.0 %reduce-scatter.13.cloned.1.call-done = f32[32,64]{1,0:T(8,128)} async-done(((f32[256,64]{1,0:T(8,128)}), f32[32,64]{1,0:T(8,128)}) %reduce-scatter.13.cloned.1.call-update) | async-done | bytes 8208
  190.3 1.2 fusion.2
  191.5 1.0 copy-done.1
  193.6 149.4 %all-reduce.8.cloned.1.call-done = f32[2,64,2048]{2,1,0:T(8,128)} async-done(((f32[2,64,2048]{2,1,0:T(8,128)}), f32[2,64,2048]{2,1,0:T(8,128)}) %all-reduce.8.cloned.1.call-update) | async-done | bytes 1048592 | tf_op jit(solution)/shard_map/psum | solution.py:54
  343.1 1.0 fusion.56
  344.0 1.0 convolution_bitcast_fusion.6
  345.8 26.0 %reduce-scatter.15.cloned.1.call-done = f32[64,64]{1,0:T(8,128)} async-done(((f32[512,64]{1,0:T(8,128)}), f32[64,64]{1,0:T(8,128)}) %reduce-scatter.15.cloned.1.call-update) | async-done | bytes 16400
  372.9 1.3 fusion.1
  374.2 1.3 copy-done
  375.7 1.3 slice-done.1
  377.7 150.7 %all-reduce.10.cloned.1.call-done = f32[4,64,2048]{2,1,0:T(8,128)} async-done(((f32[4,64,2048]{2,1,0:T(8,128)}), f32[4,64,2048]{2,1,0:T(8,128)}) %all-reduce.10.cloned.1.call-update) | async-done | bytes 2097168 | tf_op jit(solution)/shard_map/psum | solution.py:54
  528.4 1.0 fusion.57
  529.3 1.3 convolution_bitcast_fusion.7
  531.5 25.5 %reduce-scatter.9.cloned.1.call-done = f32[64,128]{1,0:T(8,128)} async-done(((f32[64,1024]{1,0:T(8,128)}), f32[64,128]{1,0:T(8,128)}) %reduce-scatter.9.cloned.1.call-update) | async-done | bytes 32784 | tf_op jit(solution)/shard_map/reduce_scatter | solution.py:37
  557.0 2.5 broadcast_in_dim.164
  559.4 1.3 fusion
  560.8 4.6 slice.54
  565.4 6.4 copy.26
  571.8 146.6 %all-reduce.12.cloned.1.call-done = f32[8,64,2048]{2,1,0:T(8,128)} async-done(((f32[8,64,2048]{2,1,0:T(8,128)}), f32[8,64,2048]{2,1,0:T(8,128)}) %all-reduce.12.cloned.1.call-update) | async-done | bytes 4194320 | tf_op jit(solution)/shard_map/psum | solution.py:54
  718.4 1.0 fusion.58
  719.4 4.4 convolution_bitcast_fusion.1
  724.4 25.9 %reduce-scatter.11.cloned.1.call-done = f32[64,256]{1,0:T(8,128)} async-done(((f32[64,2048]{1,0:T(8,128)}), f32[64,256]{1,0:T(8,128)}) %reduce-scatter.11.cloned.1.call-update) | async-done | bytes 65552 | tf_op jit(solution)/shard_map/reduce_scatter | solution.py:37
  750.4 4.3 broadcast_in_dim.169
  754.6 1.6 fusion.3
  757.1 1.0 dynamic-slice_dynamic-update-slice_fusion.4
  758.1 1.0 dynamic-slice_dynamic-update-slice_fusion.3
  759.1 1.0 dynamic-slice_dynamic-update-slice_fusion.2
  760.0 159.6 %all-reduce.14.cloned.1.call-done = f32[16,64,2048]{2,1,0:T(8,128)} async-done(((f32[16,64,2048]{2,1,0:T(8,128)}), f32[16,64,2048]{2,1,0:T(8,128)}) %all-reduce.14.cloned.1.call-update) | async-done | bytes 8388624 | tf_op jit(solution)/shard_map/psum | solution.py:54
  (52 shorter events, 10.1 us)
Async XLA Ops:
  6.5 183.7 %copy-start.2 = (f32[1,64,496]{2,1,0:T(8,128)S(1)}, f32[1,64,496]{2,1,0:T(8,128)}, u32[]{:S(2)}) copy-start(f32[1,64,496]{2,1,0:T(8,128)} %param.4) | copy-start | bytes 380932
  6.5 154.1 %all-reduce.6.cloned.1.call-start = ((), (), s32[]{:S(2)}) async-start(), calls=%async_computation.4 | async-start | bytes 1048576 | tf_op jit(solution)/shard_map/psum | solution.py:54
  10.6 178.7 %reduce-scatter.13.cloned.1.call-start = ((), (), s32[]{:S(2)}) async-start(), calls=%async_computation.11 | async-start | bytes 147456
  162.5 30.1 %slice-start = ((bf16[1,256,12544]{2,1,0:T(8,128)(2,1)}), bf16[1,256,1024]{2,1,0:T(8,128)(2,1)S(1)}, s32[]{:S(2)}) async-start(bf16[1,256,12544]{2,1,0:T(8,128)(2,1)} %param.5), calls=%async_computation.13 | async-start | bytes 1048576 | tf_op jit(solution)/shard_map/slice | solution.py:31
  162.5 180.6 %all-reduce.8.cloned.1.call-start = ((), (), s32[]{:S(2)}) async-start(), calls=%async_computation.5 | async-start | bytes 2097152 | tf_op jit(solution)/shard_map/psum | solution.py:54
  191.5 1.0 copy-start.1
  192.5 179.3 %reduce-scatter.15.cloned.1.call-start = ((), (), s32[]{:S(2)}) async-start(), calls=%async_computation.12 | async-start | bytes 294912
  345.1 183.3 %all-reduce.10.cloned.1.call-start = ((), (), s32[]{:S(2)}) async-start(), calls=%async_computation.6 | async-start | bytes 4194304 | tf_op jit(solution)/shard_map/psum | solution.py:54
  374.2 1.4 copy-start
  375.6 1.4 slice-start.1
  375.6 181.4 %reduce-scatter.9.cloned.1.call-start = ((), (), s32[]{:S(2)}) async-start(), calls=%async_computation.7 | async-start | bytes 294912 | tf_op jit(solution)/shard_map/reduce_scatter | solution.py:37
  530.7 187.7 %all-reduce.12.cloned.1.call-start = ((), (), s32[]{:S(2)}) async-start(), calls=%async_computation.8 | async-start | bytes 8388608 | tf_op jit(solution)/shard_map/psum | solution.py:54
  531.4 28.0 %copy-start.3 = (bf16[1,496,2048]{2,1,0:T(8,128)(2,1)S(1)}, bf16[1,496,2048]{2,1,0:T(8,128)(2,1)}, u32[]{:S(2)}) copy-start(bf16[1,496,2048]{2,1,0:T(8,128)(2,1)} %param.6) | copy-start | bytes 6094852
  556.9 2.5 copy-start.6
  560.7 189.6 %reduce-scatter.11.cloned.1.call-start = ((), (), s32[]{:S(2)}) async-start(), calls=%async_computation.9 | async-start | bytes 589824 | tf_op jit(solution)/shard_map/reduce_scatter | solution.py:37
  723.7 195.9 %all-reduce.14.cloned.1.call-start = ((), (), s32[]{:S(2)}) async-start(), calls=%async_computation.10 | async-start | bytes 16777216 | tf_op jit(solution)/shard_map/psum | solution.py:54
  750.4 4.3 copy-start.5
  920.7 0.7 copy-start.4
Sparse Core Ops, SparseCore 0:
  12.1 148.5 all-reduce.5
  163.1 26.1 reduce-scatter.12
  194.2 148.8 all-reduce.7
  345.4 26.3 reduce-scatter.14
  376.5 151.8 all-reduce.9
  530.8 26.1 reduce-scatter.8
  562.6 155.7 all-reduce.11
  723.9 26.4 reduce-scatter.10
  756.4 163.2 all-reduce.13
where the time goes:
time: 929 us; the launch traced here: 928 us
  waiting for transfers between devices  860 us (93%)
  local copies, waits for them, and re-layouts  33.5 us (4%)
  matrix products  15.8 us (2%)
  between operations  13.5 us (1%)
    psum x5, waiting for transfers between devices, per_device(): summed = lax.psum(slots, ('leaf', 'panel'))  756 us
    unnamed x11, waiting for transfers between devices  52.2 us
    reduce_scatter x2, waiting for transfers between devices, per_device(): lax.psum_scatter(partial_value, 'panel', scatter_dimension=1, tiled=True)  51.4 us
  transfers between devices with their start and end apart: 9, of which 9 were waited for; matrix products, arithmetic and copies ran while one was open for 2% of the time, Pallas kernels for 0%

commit v1 on v0

--- a/solution.py
+++ b/solution.py
@@ -51,7 +51,7 @@
         terms = jnp.dot(resid_low, factor, preferred_element_type=jnp.float32)
         slots = jnp.zeros((leaf_count // group_size,) + terms.shape, jnp.float32)
         slots = lax.dynamic_update_index_in_dim(slots, terms, front_pos, 0)
-        summed = lax.psum(slots, ("leaf", "panel"))
+        summed = lax.psum(lax.psum(slots, "panel"), "leaf")
         total = lax.dynamic_index_in_dim(summed, front_pos, 0, keepdims=False)
         mine = lax.dynamic_slice_in_dim(total, panel_pos * strip, strip, 1)
         rows_now = mine.astype(jnp.bfloat16)

time: 929 us -> 1060 us (1.14)
  waiting for transfers between devices: 860 us -> 988 us
    psum x5 -> x10, waiting for transfers between devices: 756 us -> 876 us  [per_device(): summed = lax.psum(lax.psum(slots, 'panel'), 'leaf')]
    unnamed x11 -> x16, waiting for transfers between devices: 52.2 us -> 56.2 us
  transfers between devices with their start and end apart: 9 -> 14, of which waited for: 9 -> 14; matrix products, arithmetic and copies ran while one was open for 2% -> 2% of each run, Pallas kernels for 0% -> 0%
where the time goes in v1:
time: 1060 us
  waiting for transfers between devices  988 us (93%)
  local copies, waits for them, and re-layouts  33.5 us (3%)
  matrix products  15.9 us (2%)
  between operations  13.6 us (1%)
    psum x10, waiting for transfers between devices, per_device(): summed = lax.psum(lax.psum(slots, 'panel'), 'leaf')  876 us
    unnamed x16, waiting for transfers between devices  56.2 us
    reduce_scatter x2, waiting for transfers between devices, per_device(): lax.psum_scatter(partial_value, 'panel', scatter_dimension=1, tiled=True)  55.2 us
  transfers between devices with their start and end apart: 14, of which 14 were waited for; matrix products, arithmetic and copies ran while one was open for 2% of the time, Pallas kernels for 0%

profile of v1, /device:TPU:1, one launch (start us, length us, event | category | flops | bytes accessed | tf_op | source)
XLA Modules:
  0.0 1055.8 jit_solution(15179322652996174035)
XLA Ops:
  6.5 1.5 fusion.88
  8.7 1.9 convolution_bitcast_fusion
  10.7 62.1 %all-reduce.11.cloned.1.call-done = f32[1,64,2048]{2,1,0:T(8,128)} async-done(((f32[1,64,2048]{2,1,0:T(8,128)}), f32[1,64,2048]{2,1,0:T(8,128)}) %all-reduce.11.cloned.1.call-update) | async-done | bytes 524304 | tf_op jit(solution)/shard_map/psum | solution.py:54
  72.8 88.7 %all-reduce.13.cloned.1.call-done = f32[1,64,2048]{2,1,0:T(8,128)} async-done(((f32[1,64,2048]{2,1,0:T(8,128)}), f32[1,64,2048]{2,1,0:T(8,128)}) %all-reduce.13.cloned.1.call-update) | async-done | bytes 524304 | tf_op jit(solution)/shard_map/psum | solution.py:54
  161.5 1.8 convolution_bitcast_fusion.8
  164.1 27.9 %reduce-scatter.13.cloned.1.call-done = f32[32,64]{1,0:T(8,128)} async-done(((f32[256,64]{1,0:T(8,128)}), f32[32,64]{1,0:T(8,128)}) %reduce-scatter.13.cloned.1.call-update) | async-done | bytes 8208
  193.0 1.3 fusion.2
  194.3 1.0 copy-done.1
  195.3 62.1 %all-reduce.15.cloned.1.call-done = f32[2,64,2048]{2,1,0:T(8,128)} async-done(((f32[2,64,2048]{2,1,0:T(8,128)}), f32[2,64,2048]{2,1,0:T(8,128)}) %all-reduce.15.cloned.1.call-update) | async-done | bytes 1048592 | tf_op jit(solution)/shard_map/psum | solution.py:54
  258.6 89.3 %all-reduce.17.cloned.1.call-done = f32[2,64,2048]{2,1,0:T(8,128)} async-done(((f32[2,64,2048]{2,1,0:T(8,128)}), f32[2,64,2048]{2,1,0:T(8,128)}) %all-reduce.17.cloned.1.call-update) | async-done | bytes 1048592 | tf_op jit(solution)/shard_map/psum | solution.py:54
  348.9 1.0 convolution_bitcast_fusion.6
  350.7 28.1 %reduce-scatter.15.cloned.1.call-done = f32[64,64]{1,0:T(8,128)} async-done(((f32[512,64]{1,0:T(8,128)}), f32[64,64]{1,0:T(8,128)}) %reduce-scatter.15.cloned.1.call-update) | async-done | bytes 16400
  379.8 1.3 fusion.1
  381.1 1.3 copy-done
  382.5 65.4 %all-reduce.19.cloned.1.call-done = f32[4,64,2048]{2,1,0:T(8,128)} async-done(((f32[4,64,2048]{2,1,0:T(8,128)}), f32[4,64,2048]{2,1,0:T(8,128)}) %all-reduce.19.cloned.1.call-update) | async-done | bytes 2097168 | tf_op jit(solution)/shard_map/psum | solution.py:54
  448.0 1.3 slice-done.1
  450.0 92.0 %all-reduce.21.cloned.1.call-done = f32[4,64,2048]{2,1,0:T(8,128)} async-done(((f32[4,64,2048]{2,1,0:T(8,128)}), f32[4,64,2048]{2,1,0:T(8,128)}) %all-reduce.21.cloned.1.call-update) | async-done | bytes 2097168 | tf_op jit(solution)/shard_map/psum | solution.py:54
  543.0 1.3 convolution_bitcast_fusion.7
  545.1 27.6 %reduce-scatter.9.cloned.1.call-done = f32[64,128]{1,0:T(8,128)} async-done(((f32[64,1024]{1,0:T(8,128)}), f32[64,128]{1,0:T(8,128)}) %reduce-scatter.9.cloned.1.call-update) | async-done | bytes 32784 | tf_op jit(solution)/shard_map/reduce_scatter | solution.py:37
  572.7 2.5 broadcast_in_dim.164
  575.2 1.3 fusion
  576.5 72.4 %all-reduce.23.cloned.1.call-done = f32[8,64,2048]{2,1,0:T(8,128)} async-done(((f32[8,64,2048]{2,1,0:T(8,128)}), f32[8,64,2048]{2,1,0:T(8,128)}) %all-reduce.23.cloned.1.call-update) | async-done | bytes 4194320 | tf_op jit(solution)/shard_map/psum | solution.py:54
  649.0 4.6 slice.54
  653.6 6.4 copy.26
  660.0 97.5 %all-reduce.25.cloned.1.call-done = f32[8,64,2048]{2,1,0:T(8,128)} async-done(((f32[8,64,2048]{2,1,0:T(8,128)}), f32[8,64,2048]{2,1,0:T(8,128)}) %all-reduce.25.cloned.1.call-update) | async-done | bytes 4194320 | tf_op jit(solution)/shard_map/psum | solution.py:54
  758.5 4.4 convolution_bitcast_fusion.1
  763.5 27.6 %reduce-scatter.11.cloned.1.call-done = f32[64,256]{1,0:T(8,128)} async-done(((f32[64,2048]{1,0:T(8,128)}), f32[64,256]{1,0:T(8,128)}) %reduce-scatter.11.cloned.1.call-update) | async-done | bytes 65552 | tf_op jit(solution)/shard_map/reduce_scatter | solution.py:37
  791.1 4.3 broadcast_in_dim.169
  795.4 1.6 fusion.3
  797.0 105.2 %all-reduce.27.cloned.1.call-done = f32[16,64,2048]{2,1,0:T(8,128)} async-done(((f32[16,64,2048]{2,1,0:T(8,128)}), f32[16,64,2048]{2,1,0:T(8,128)}) %all-reduce.27.cloned.1.call-update) | async-done | bytes 8388624 | tf_op jit(solution)/shard_map/psum | solution.py:54
  905.1 1.0 dynamic-slice_dynamic-update-slice_fusion.2
  906.0 141.6 %all-reduce.29.cloned.1.call-done = f32[16,64,2048]{2,1,0:T(8,128)} async-done(((f32[16,64,2048]{2,1,0:T(8,128)}), f32[16,64,2048]{2,1,0:T(8,128)}) %all-reduce.29.cloned.1.call-update) | async-done | bytes 8388624 | tf_op jit(solution)/shard_map/psum | solution.py:54
  (67 shorter events, 15.2 us)
Async XLA Ops:
  6.5 186.4 %copy-start.2 = (f32[1,64,496]{2,1,0:T(8,128)S(1)}, f32[1,64,496]{2,1,0:T(8,128)}, u32[]{:S(2)}) copy-start(f32[1,64,496]{2,1,0:T(8,128)} %param.4) | copy-start | bytes 380932
  6.5 66.2 %all-reduce.11.cloned.1.call-start = ((), (), s32[]{:S(2)}) async-start(), calls=%async_computation.4 | async-start | bytes 1048576 | tf_op jit(solution)/shard_map/psum | solution.py:54
  10.6 150.8 %all-reduce.13.cloned.1.call-start = ((), (), s32[]{:S(2)}) async-start(), calls=%async_computation.5 | async-start | bytes 1048576 | tf_op jit(solution)/shard_map/psum | solution.py:54
  72.8 119.3 %reduce-scatter.13.cloned.1.call-start = ((), (), s32[]{:S(2)}) async-start(), calls=%async_computation.16 | async-start | bytes 147456
  163.3 94.1 %all-reduce.15.cloned.1.call-start = ((), (), s32[]{:S(2)}) async-start(), calls=%async_computation.6 | async-start | bytes 2097152 | tf_op jit(solution)/shard_map/psum | solution.py:54
  193.0 64.6 %slice-start = ((bf16[1,256,12544]{2,1,0:T(8,128)(2,1)}), bf16[1,256,1024]{2,1,0:T(8,128)(2,1)S(1)}, s32[]{:S(2)}) async-start(bf16[1,256,12544]{2,1,0:T(8,128)(2,1)} %param.5), calls=%async_computation.18 | async-start | bytes 1048576 | tf_op jit(solution)/shard_map/slice | solution.py:31
  194.2 1.0 copy-start.1
  195.3 152.7 %all-reduce.17.cloned.1.call-start = ((), (), s32[]{:S(2)}) async-start(), calls=%async_computation.7 | async-start | bytes 2097152 | tf_op jit(solution)/shard_map/psum | solution.py:54
  257.5 121.2 %reduce-scatter.15.cloned.1.call-start = ((), (), s32[]{:S(2)}) async-start(), calls=%async_computation.17 | async-start | bytes 294912
  349.9 97.9 %all-reduce.19.cloned.1.call-start = ((), (), s32[]{:S(2)}) async-start(), calls=%async_computation.8 | async-start | bytes 4194304 | tf_op jit(solution)/shard_map/psum | solution.py:54
  381.1 1.3 copy-start
  382.4 159.6 %all-reduce.21.cloned.1.call-start = ((), (), s32[]{:S(2)}) async-start(), calls=%async_computation.9 | async-start | bytes 4194304 | tf_op jit(solution)/shard_map/psum | solution.py:54
  447.9 1.4 slice-start.1
  447.9 124.8 %reduce-scatter.9.cloned.1.call-start = ((), (), s32[]{:S(2)}) async-start(), calls=%async_computation.10 | async-start | bytes 294912 | tf_op jit(solution)/shard_map/reduce_scatter | solution.py:37
  544.3 104.7 %all-reduce.23.cloned.1.call-start = ((), (), s32[]{:S(2)}) async-start(), calls=%async_computation.11 | async-start | bytes 8388608 | tf_op jit(solution)/shard_map/psum | solution.py:54
  545.0 30.1 %copy-start.3 = (bf16[1,496,2048]{2,1,0:T(8,128)(2,1)S(1)}, bf16[1,496,2048]{2,1,0:T(8,128)(2,1)}, u32[]{:S(2)}) copy-start(bf16[1,496,2048]{2,1,0:T(8,128)(2,1)} %param.6) | copy-start | bytes 6094852
  572.7 2.5 copy-start.6
  576.5 181.0 %all-reduce.25.cloned.1.call-start = ((), (), s32[]{:S(2)}) async-start(), calls=%async_computation.12 | async-start | bytes 8388608 | tf_op jit(solution)/shard_map/psum | solution.py:54
  649.0 142.1 %reduce-scatter.11.cloned.1.call-start = ((), (), s32[]{:S(2)}) async-start(), calls=%async_computation.13 | async-start | bytes 589824 | tf_op jit(solution)/shard_map/reduce_scatter | solution.py:37
  762.8 139.4 %all-reduce.27.cloned.1.call-start = ((), (), s32[]{:S(2)}) async-start(), calls=%async_computation.14 | async-start | bytes 16777216 | tf_op jit(solution)/shard_map/psum | solution.py:54
  791.1 4.3 copy-start.5
  797.0 250.6 %all-reduce.29.cloned.1.call-start = ((), (), s32[]{:S(2)}) async-start(), calls=%async_computation.15 | async-start | bytes 16777216 | tf_op jit(solution)/shard_map/psum | solution.py:54
  1048.6 0.7 copy-start.4
Sparse Core Ops, SparseCore 0:
  10.8 61.9 all-reduce.10
  76.3 85.1 all-reduce.12
  163.8 28.1 reduce-scatter.12
  195.4 62.0 all-reduce.14
  260.9 87.0 all-reduce.16
  350.3 28.3 reduce-scatter.14
  382.6 65.2 all-reduce.18
  451.2 90.7 all-reduce.20
  544.5 28.1 reduce-scatter.8
  576.6 72.2 all-reduce.22
  652.3 105.1 all-reduce.24
  763.0 28.0 reduce-scatter.10
  797.1 105.0 all-reduce.26
  906.1 141.4 all-reduce.28
